TPU v7x, 256 devices: a whole 4x4x8 slice. The times are simulated.
256 devices in a mesh: req: 32 (over x, z_hi, core), tp: 8 (over y, z_lo).
Axes of the slice: x: 4, y: 4, z: 8 (z_hi: 4, z_lo: 2; z = z_hi * 2 + z_lo), core: 2. Of those that a mesh axis runs over, the one named last changes fastest.
Arguments:
- queries: bfloat16 [8192, 5120], P('req', 'tp')
- suffix_keys: bfloat16 [8192, 5120], P('req', 'tp')
- suffix_values: bfloat16 [8192, 5120], P('req', 'tp'), may hold values from -6 to 6
- page_cache: bfloat16 [64, 128, 2, 5120], P('req', None, None, 'tp'), may hold values from -6 to 6
- page_table: int32 [2, 32], replicated, may hold values from 0 to 63, as said below
- suffix_lengths: int32 [32, 4], P('req'), may hold values from 1 to 128, 256 in all within a row
- request_group: int32 [32, 4], P('req'), may hold values from 0 to 1
- residual: bfloat16 [8192, 5120], P('req', 'tp'), may hold values from -6 to 6
- out_weight: bfloat16 [5120, 5120], P('tp'), may hold values from -0.3125 to 0.3125
- attn_gate: float32 [5120], P('tp'), may hold values from 0.5 to 2
- mod_shift: float32 [5120], P('tp'), may hold values from -3 to 3
- mod_scale: float32 [5120], P('tp'), may hold values from -0.5 to 1
Outputs:
- stream: bfloat16 [8192, 5120], P('req', 'tp')
- mlp_input: bfloat16 [8192, 5120], P('req', 'tp')
Inputs may be any that keep to these rules, and one draw needn't show every extreme that they name: `page_table`: every slot 0 to 63 appears exactly once; slot s lies on req index s // 2. `suffix_lengths`: the lengths of one req index's requests sum to 256.
All inputs are finite; a program needn't handle non-finite values.
Results may differ from a plain program's by a relative error of at most 0.015.
Values may be sent and summed in bfloat16 or wider, within the bound.
No kernel may reach another device: no remote copies, remote signals or barrier semaphores. Data moves between devices by JAX's collectives and lax.ppermute only.
A program may use at most 128 MiB of HBM per device.

v0:
```python
import math
import jax
import jax.numpy as jnp
from jax import lax
from jax.sharding import PartitionSpec as P

D = 5120
HS = 128
SPAN = 64


def body(
    queries,
    suffix_keys,
    suffix_values,
    page_cache,
    page_table,
    suffix_lengths,
    request_group,
    residual,
    out_weight,
    attn_gate,
    mod_shift,
    mod_scale,
):
    tok_count = queries.shape[0]
    local_heads = queries.shape[1] // HS
    page_size = page_cache.shape[1]
    group_count = page_table.shape[0]
    page_count = page_table.shape[1]
    slot_total = group_count * page_count
    inv_sqrt = 1.0 / math.sqrt(HS)
    slot_ids = jnp.arange(slot_total, dtype=jnp.int32)
    table_group = jnp.arange(slot_total, dtype=jnp.int32) // page_count
    matches = page_table.reshape(-1)[:, None] == slot_ids[None, :]
    slot_group = jnp.sum(jnp.where(matches, table_group[:, None], 0), 0)
    positions = jnp.arange(tok_count, dtype=jnp.int32)
    lengths_row = suffix_lengths[0]
    request_ends = jnp.cumsum(lengths_row, dtype=jnp.int32)
    request_starts = request_ends - lengths_row
    token_request = jnp.sum((positions[:, None] >= request_ends[None, :]).astype(jnp.int32), 1)
    choose = token_request[:, None] == jnp.arange(suffix_lengths.shape[1], dtype=jnp.int32)[None, :]
    token_group = jnp.sum(jnp.where(choose, request_group[0][None, :], 0), 1)
    token_start = jnp.sum(jnp.where(choose, request_starts[None, :], 0), 1)
    token_block = (positions - token_start) // SPAN
    query_heads = queries.reshape(tok_count, local_heads, HS)
    key_heads = suffix_keys.reshape(tok_count, local_heads, HS)
    value_heads = suffix_values.reshape(tok_count, local_heads, HS)
    same_request = (token_request[:, None] == token_request[None, :]) & (
        token_block[None, :] <= token_block[:, None]
    )
    scores = (
        jnp.einsum("qhd,khd->hqk", query_heads, key_heads, preferred_element_type=jnp.float32)
        * inv_sqrt
    )
    scores = jnp.where(same_request[None], scores, -1e30)
    largest = jnp.max(scores, -1)
    expo = jnp.where(same_request[None], jnp.exp(scores - largest[..., None]), 0.0)
    denominator = jnp.sum(expo, -1)
    weighted = jnp.einsum(
        "hqk,khd->hqd", expo.astype(jnp.bfloat16), value_heads, preferred_element_type=jnp.float32
    )
    own_state = (largest, denominator, weighted)
    shard_block = lax.all_gather(page_cache, "req", axis=0, tiled=True)
    slot_number = shard_block.shape[0]
    step = math.gcd(slot_number, 4)
    block_count = slot_number // step
    blocks = shard_block.reshape(block_count, step, page_size, 2, local_heads * HS)
    block_starts = step * jnp.arange(block_count, dtype=jnp.int32)

    def one_block(carried, item):
        block, block_start = item
        key_rows = block[:, :, 0, :].reshape(step * page_size, local_heads, HS)
        value_rows = block[:, :, 1, :].reshape(step * page_size, local_heads, HS)
        key_group = jnp.repeat(lax.dynamic_slice_in_dim(slot_group, block_start, step), page_size)
        visible = token_group[:, None] == key_group[None, :]
        max_old, sum_old, acc_old = carried
        page_scores = (
            jnp.einsum("qhd,khd->hqk", query_heads, key_rows, preferred_element_type=jnp.float32)
            * inv_sqrt
        )
        page_scores = jnp.where(visible[None], page_scores, -1e30)
        max_new = jnp.maximum(max_old, jnp.max(page_scores, -1))
        page_expo = jnp.where(visible[None], jnp.exp(page_scores - max_new[..., None]), 0.0)
        factor = jnp.exp(max_old - max_new)
        sum_new = sum_old * factor + jnp.sum(page_expo, -1)
        acc_new = acc_old * factor[..., None] + jnp.einsum(
            "hqk,khd->hqd",
            page_expo.astype(jnp.bfloat16),
            value_rows,
            preferred_element_type=jnp.float32,
        )
        return ((max_new, sum_new, acc_new), None)

    result, unused = lax.scan(one_block, own_state, (blocks, block_starts))
    max_all, sum_all, acc_all = result
    attention = (
        (acc_all / sum_all[..., None])
        .transpose(1, 0, 2)
        .reshape(tok_count, local_heads * HS)
        .astype(jnp.bfloat16)
    )
    projected = (
        lax.psum_scatter(
            lax.dot_general(
                out_weight, attention, (((0,), (1,)), ((), ())), preferred_element_type=jnp.float32
            ).astype(jnp.bfloat16),
            "tp",
            scatter_dimension=0,
            tiled=True,
        )
        .astype(jnp.float32)
        .T
    )
    combined = residual.astype(jnp.float32) + attn_gate[None, :] * projected
    sum_first, sum_second = lax.psum((jnp.sum(combined, 1), jnp.sum(combined * combined, 1)), "tp")
    mean_value = sum_first / D
    variance = sum_second / D - mean_value * mean_value
    normed = (combined - mean_value[:, None]) / jnp.sqrt(variance[:, None] + 1e-06)
    mlp_input = normed * (1.0 + mod_scale[None, :]) + mod_shift[None, :]
    return (combined.astype(jnp.bfloat16), mlp_input.astype(jnp.bfloat16))


def solution(mesh):
    in_specs = (
        P("req", "tp"),
        P("req", "tp"),
        P("req", "tp"),
        P("req", None, None, "tp"),
        P(),
        P("req", None),
        P("req", None),
        P("req", "tp"),
        P("tp", None),
        P("tp"),
        P("tp"),
        P("tp"),
    )
    out_specs = (P("req", "tp"), P("req", "tp"))
    return jax.shard_map(body, mesh=mesh, in_specs=in_specs, out_specs=out_specs, check_vma=False)
```

profile of v0, /device:TPU:2, one launch (start us, length us, event | category | flops | bytes accessed | tf_op | source)
XLA Modules:
  0.0 477.4 jit_solution(15765563890964449459)
XLA Ops:
  7.3 2.1 copy.68
  15.2 128.3 %all-gather.2.cloned.1.call-done = bf16[64,128,2,640]{3,1,2,0:T(8,128)(2,1)} async-done(((bf16[2,128,2,640]{3,1,2,0:T(8,128)(2,1)}), bf16[64,128,2,640]{3,1,2,0:T(8,128)(2,1)}) %all-gather.2.cloned.1.call-update) | async-done | bytes 20971536 | tf_op jit(solution)/shard_map/all_gather | solution.py:64
  143.5 225.4 %while.14 = (s32[]{:T(128)}, f32[5,256]{1,0:T(8,128)S(1)}, f32[5,256]{1,0:T(8,128)S(1)}, f32[5,256,128]{2,1,0:T(8,128)}, s32[256]{0:T(256)S(1)}, /*index=5*/s32[...) while((s32[]{:T(128)}, f32[5,256]{1,0:T(8,128)S(1)}, ...), condition=%wide.region_10.11_spmd, body=%wide.region_7.10_spmd.sunk | while | flops 344525312 | bytes 21910748 | solution.py:95
  150.8 1.8 fusion.48
  154.4 3.2 fusion.50
  168.5 3.2 fusion.50
  182.6 3.2 fusion.50
  196.7 3.2 fusion.50
  210.7 3.2 fusion.50
  224.8 3.2 fusion.50
  238.9 3.2 fusion.50
  253.0 3.2 fusion.50
  267.1 3.2 fusion.50
  281.2 3.2 fusion.50
  295.3 3.2 fusion.50
  309.3 3.2 fusion.50
  323.4 3.2 fusion.50
  337.5 3.2 fusion.50
  351.6 3.2 fusion.50
  365.7 3.2 fusion.50
  370.2 5.1 %fusion.12 = bf16[5120,256]{0,1:T(8,128)(2,1)S(1)} fusion(bf16[256,640]{0,1:T(8,128)(2,1)S(1)} %bitcast.80, bf16[640,5120]{1,0:T(8,128)(2,1)} %param.22), kind=kOutput, calls=%fused_computation.17 | convolution fusion | flops 1679032320 | bytes 9502720 | tf_op jit(solution)/shard_map/dot_general | solution.py:105
  375.4 2.6 copy.79
  378.6 72.4 %reduce-scatter.4.cloned.1.call-done = bf16[640,256]{1,0:T(8,128)(2,1)} async-done(((bf16[5120,256]{1,0:T(8,128)(2,1)}), bf16[640,256]{1,0:T(8,128)(2,1)}) %reduce-scatter.4.cloned.1.call-update) | async-done | bytes 327696
  452.5 17.0 %all-reduce = (f32[256]{0:T(256)S(1)}, f32[256]{0:T(256)S(1)}) all-reduce(f32[256]{0:T(256)S(1)} %get-tuple-element.89, f32[256]{0:T(256)S(1)} %get-tuple-element.88), channel_id=1, replica_groups=mesh['req'=32,'tp'=8] {'tp'}, use_global_device_ids=true, to_apply=%region_15.16 | all-reduce | flops 512 | bytes 4096 | tf_op jit(solution)/shard_map/psum | solution.py:116
  (269 shorter events, 152.9 us)
Async XLA Ops:
  7.2 5.8 %copy-start.8 = (s32[1,4]{1,0:T(1,128)S(1)}, s32[1,4]{1,0:T(1,128)}, u32[]{:S(2)}) copy-start(s32[1,4]{1,0:T(1,128)} %param.19) | copy-start | bytes 52
  7.2 4.2 copy-start.1
  7.2 4.4 copy-start.2
  7.2 5.4 %copy-start.7 = (s32[2,32]{1,0:T(2,128)S(1)}, s32[2,32]{1,0:T(2,128)}, u32[]{:S(2)}) copy-start(s32[2,32]{1,0:T(2,128)} %param.18) | copy-start | bytes 772
  7.2 5.7 %copy-start.6 = (s32[1,4]{1,0:T(1,128)S(1)}, s32[1,4]{1,0:T(1,128)}, u32[]{:S(2)}) copy-start(s32[1,4]{1,0:T(1,128)} %param.20) | copy-start | bytes 52
  7.2 136.3 %all-gather.2.cloned.1.call-start = ((), (), s32[]{:S(2)}) async-start(), calls=%async_computation.1 | async-start | bytes 21626880 | tf_op jit(solution)/shard_map/all_gather | solution.py:64
  9.3 441.7 %reduce-scatter.4.cloned.1.call-start = ((), (), s32[]{:S(2)}) async-start(), calls=%async_computation.2 | async-start | bytes 2949120
  377.9 0.7 copy-start.4
  377.9 74.3 %copy-start = (bf16[256,640]{1,0:T(8,128)(2,1)S(1)}, bf16[256,640]{1,0:T(8,128)(2,1)}, u32[]{:S(2)}) copy-start(bf16[256,640]{1,0:T(8,128)(2,1)} %param.21) | copy-start | bytes 983044
  377.9 74.3 %copy-start.3 = (f32[640]{0:T(1024)S(1)}, f32[640]{0:T(1024)}, u32[]{:S(2)}) copy-start(f32[640]{0:T(1024)} %param.23) | copy-start | bytes 7684
  377.9 91.5 %copy-start.5 = (f32[640]{0:T(1024)S(1)}, f32[640]{0:T(1024)}, u32[]{:S(2)}) copy-start(f32[640]{0:T(1024)} %param.24) | copy-start | bytes 7684
Sparse Core Ops, SparseCore 0:
  10.6 132.8 all-gather.1
  378.1 72.8 reduce-scatter.3
where the time goes:
time: 479 us; the launch traced here: 477 us
  waiting for transfers between devices  201 us (42%)
  local copies, waits for them, and re-layouts  113 us (24%)
  matrix products  86.8 us (18%)
  loops' own time  30.4 us (6%)
  blocking collectives  17 us (4%)
  other arithmetic  15.7 us (3%)
  between operations  14.2 us (3%)
    all_gather x1, waiting for transfers between devices, body(): shard_block = lax.all_gather(page_cache, 'req', axis=0, tiled=True)  128 us
    unnamed x3, waiting for transfers between devices  72.4 us
    dynamic_slice x48, local copies, waits for them, and re-layouts, body(): result, unused = lax.scan(one_block, own_state, (blocks, block_starts))  57.7 us
    dot_general x16, matrix products, one_block(): jnp.einsum('hqk,khd->hqd', page_expo.astype(jnp.bfloat16), value_rows, pr...  50.7 us
    another operation x1, loops' own time, body(): result, unused = lax.scan(one_block, own_state, (blocks, block_starts))  30.4 us
    dot_general x16, matrix products, one_block(): jnp.einsum('qhd,khd->hqk', query_heads, key_rows, preferred_element_type=...  29.3 us
    squeeze x16, local copies, waits for them, and re-layouts, one_block(): key_rows = block[:, :, 0, :].reshape(step * page_size, local_heads, HS)  17.4 us
    squeeze x16, local copies, waits for them, and re-layouts, one_block(): value_rows = block[:, :, 1, :].reshape(step * page_size, local_heads, HS)  17.4 us
  transfers between devices with their start and end apart: 2, of which 2 were waited for; matrix products, arithmetic and copies ran while one was open for 1% of the time, Pallas kernels for 0%

commit v1 on v0

--- a/solution.py
+++ b/solution.py
@@ -61,7 +61,9 @@
         "hqk,khd->hqd", expo.astype(jnp.bfloat16), value_heads, preferred_element_type=jnp.float32
     )
     own_state = (largest, denominator, weighted)
-    shard_block = lax.all_gather(page_cache, "req", axis=0, tiled=True)
+    shard_block = jnp.concatenate(
+        lax.all_to_all(jnp.stack([page_cache] * lax.axis_size("req")), "req", 0, 0), axis=0
+    )
     slot_number = shard_block.shape[0]
     step = math.gcd(slot_number, 4)
     block_count = slot_number // step

time: 479 us -> 813 us (1.70)
  waiting for transfers between devices: 201 us -> 517 us
  starting transfers between devices: 0.08 us -> 11.8 us
    all_to_all x0 -> x1, waiting for transfers between devices: none -> 448 us  [body(): lax.all_to_all(jnp.stack([page_cache] * lax.axis_size('req')), 'req', 0, 0)]
    all_gather x1 -> x0, waiting for transfers between devices: 128 us -> none  [body(): shard_block = lax.all_gather(page_cache, 'req', axis=0, tiled=True)]
    all_to_all x0 -> x1, starting transfers between devices: none -> 11.8 us  [body(): lax.all_to_all(jnp.stack([page_cache] * lax.axis_size('req')), 'req', 0, 0)]
    unnamed x3 -> x2, waiting for transfers between devices: 72.4 us -> 68.7 us
where the time goes in v1:
time: 813 us; the launch traced here: 811 us
  waiting for transfers between devices  517 us (64%)
  local copies, waits for them, and re-layouts  119 us (15%)
  matrix products  87.1 us (11%)
  loops' own time  30.4 us (4%)
  blocking collectives  17 us (2%)
  other arithmetic  15 us (2%)
  between operations  14.2 us (2%)
  starting transfers between devices  11.8 us (1%)
    all_to_all x1, waiting for transfers between devices, body(): lax.all_to_all(jnp.stack([page_cache] * lax.axis_size('req')), 'req', 0, 0)  448 us
    unnamed x2, waiting for transfers between devices  68.7 us
    dynamic_slice x48, local copies, waits for them, and re-layouts, body(): result, unused = lax.scan(one_block, own_state, (blocks, block_starts))  57.7 us
    dot_general x16, matrix products, one_block(): jnp.einsum('hqk,khd->hqd', page_expo.astype(jnp.bfloat16), value_rows, pr...  50.9 us
    another operation x1, loops' own time, body(): result, unused = lax.scan(one_block, own_state, (blocks, block_starts))  30.4 us
    dot_general x16, matrix products, one_block(): jnp.einsum('qhd,khd->hqk', query_heads, key_rows, preferred_element_type=...  29.3 us
    squeeze x16, local copies, waits for them, and re-layouts, one_block(): key_rows = block[:, :, 0, :].reshape(step * page_size, local_heads, HS)  17.4 us
    squeeze x16, local copies, waits for them, and re-layouts, one_block(): value_rows = block[:, :, 1, :].reshape(step * page_size, local_heads, HS)  17.4 us
  transfers between devices with their start and end apart: 2, of which 2 were waited for; matrix products, arithmetic and copies ran while one was open for 1% of the time, Pallas kernels for 0%

profile of v1, /device:TPU:2, one launch (start us, length us, event | category | flops | bytes accessed | tf_op | source)
XLA Modules:
  0.0 811.4 jit_solution(14619319780856494959)
XLA Ops:
  8.3 8.1 %stack.2 = bf16[32,2,128,2,640]{4,2,3,1,0:T(8,128)(2,1)} broadcast(bf16[2,128,2,640]{3,1,2,0:T(8,128)(2,1)S(1)} %copy.68), dimensions={1,2,3,4} | broadcast | bytes 21626880 | tf_op jit(solution)/shard_map/stack | solution.py:65
  16.5 11.8 %all-to-all-start = ((bf16[32,2,128,2,640]{4,2,3,1,0:T(8,128)(2,1)}), bf16[32,2,128,2,640]{4,2,3,1,0:T(8,128)(2,1)}, u32[]{:S(2)}, u32[]{:S(2)}) async-start(bf16[32,2,128,2,640]{4,2,3,1,0:T(8,128)(2,1)} %stack.2), calls=%async_computation | async-start | bytes 41943040 | tf_op jit(solution)/shard_map/all_to_all | solution.py:65
  32.6 448.4 %all-to-all-done = bf16[32,2,128,2,640]{4,2,3,1,0:T(8,128)(2,1)} async-done(((bf16[32,2,128,2,640]{4,2,3,1,0:T(8,128)(2,1)}), bf16[32,2,128,2,640]{4,2,3,1,0:T(8,128)(2,1)}, u32[]{:S(2)}, u32[]{:S(2)}) %all-to-all-start) | async-done | bytes 20971552 | tf_op jit(solution)/shard_map/all_to_all | solution.py:65
  481.0 225.6 %while.14 = (s32[]{:T(128)}, f32[5,256]{1,0:T(8,128)S(1)}, f32[5,256]{1,0:T(8,128)S(1)}, f32[5,256,128]{2,1,0:T(8,128)}, s32[256]{0:T(256)S(1)}, /*index=5*/s32[...) while((s32[]{:T(128)}, f32[5,256]{1,0:T(8,128)S(1)}, ...), condition=%wide.region_10.11_spmd, body=%wide.region_7.10_spmd.sunk | while | flops 344525312 | bytes 21910748 | solution.py:97
  491.9 3.2 fusion.50
  506.0 3.2 fusion.50
  520.1 3.2 fusion.50
  534.2 3.2 fusion.50
  548.3 3.2 fusion.50
  562.4 3.2 fusion.50
  576.5 3.2 fusion.50
  590.6 3.2 fusion.50
  604.7 3.2 fusion.50
  618.8 3.2 fusion.50
  632.9 3.2 fusion.50
  647.0 3.2 fusion.50
  661.1 3.2 fusion.50
  675.2 3.2 fusion.50
  689.3 3.2 fusion.50
  703.4 3.2 fusion.50
  707.9 5.1 fusion.12
  713.1 2.6 copy.79
  716.3 68.7 %reduce-scatter.4.cloned.1.call-done = bf16[640,256]{1,0:T(8,128)(2,1)} async-done(((bf16[5120,256]{1,0:T(8,128)(2,1)}), bf16[640,256]{1,0:T(8,128)(2,1)}) %reduce-scatter.4.cloned.1.call-update) | async-done | bytes 327696
  786.5 17.0 %all-reduce = (f32[256]{0:T(256)S(1)}, f32[256]{0:T(256)S(1)}) all-reduce(f32[256]{0:T(256)S(1)} %get-tuple-element.89, f32[256]{0:T(256)S(1)} %get-tuple-element.88), channel_id=1, replica_groups=mesh['req'=32,'tp'=8] {'tp'}, use_global_device_ids=true, to_apply=%region_15.16 | all-reduce | flops 512 | bytes 4096 | tf_op jit(solution)/shard_map/psum | solution.py:118
  (271 shorter events, 154.2 us)
Async XLA Ops:
  16.4 11.9 %copy-start.9 = (s32[1,4]{1,0:T(1,128)S(1)}, s32[1,4]{1,0:T(1,128)}, u32[]{:S(2)}) copy-start(s32[1,4]{1,0:T(1,128)} %param.19) | copy-start | bytes 52
  16.4 12.1 %copy-start.1 = (bf16[256,640]{1,0:T(8,128)(2,1)S(1)}, bf16[256,640]{1,0:T(8,128)(2,1)}, u32[]{:S(2)}) copy-start(bf16[256,640]{1,0:T(8,128)(2,1)} %param.14) | copy-start | bytes 983044
  16.5 12.3 %copy-start.2 = (bf16[256,640]{1,0:T(8,128)(2,1)S(1)}, bf16[256,640]{1,0:T(8,128)(2,1)}, u32[]{:S(2)}) copy-start(bf16[256,640]{1,0:T(8,128)(2,1)} %param.15) | copy-start | bytes 983044
  16.5 12.5 %copy-start.3 = (bf16[256,640]{1,0:T(8,128)(2,1)S(1)}, bf16[256,640]{1,0:T(8,128)(2,1)}, u32[]{:S(2)}) copy-start(bf16[256,640]{1,0:T(8,128)(2,1)} %param.16) | copy-start | bytes 983044
  16.5 464.5 %all-to-all-start = ((bf16[32,2,128,2,640]{4,2,3,1,0:T(8,128)(2,1)}), bf16[32,2,128,2,640]{4,2,3,1,0:T(8,128)(2,1)}, u32[]{:S(2)}, u32[]{:S(2)}) async-start(bf16[32,2,128,2,640]{4,2,3,1,0:T(8,128)(2,1)} %stack.2), calls=%async_computation | async-start | bytes 41943040 | tf_op jit(solution)/shard_map/all_to_all | solution.py:65
  28.3 1.7 copy-start.8
  28.3 2.0 copy-start.7
  28.3 756.7 %reduce-scatter.4.cloned.1.call-start = ((), (), s32[]{:S(2)}) async-start(), calls=%async_computation.2 | async-start | bytes 2949120
  715.6 0.7 copy-start.5
  715.6 70.6 %copy-start = (bf16[256,640]{1,0:T(8,128)(2,1)S(1)}, bf16[256,640]{1,0:T(8,128)(2,1)}, u32[]{:S(2)}) copy-start(bf16[256,640]{1,0:T(8,128)(2,1)} %param.21) | copy-start | bytes 983044
  715.6 70.6 %copy-start.4 = (f32[640]{0:T(1024)S(1)}, f32[640]{0:T(1024)}, u32[]{:S(2)}) copy-start(f32[640]{0:T(1024)} %param.23) | copy-start | bytes 7684
  715.6 87.8 %copy-start.6 = (f32[640]{0:T(1024)S(1)}, f32[640]{0:T(1024)}, u32[]{:S(2)}) copy-start(f32[640]{0:T(1024)} %param.24) | copy-start | bytes 7684
Sparse Core Ops, SparseCore 0:
  715.8 69.2 reduce-scatter.3
